TPU v7x, 512 devices: a whole 4x8x8 slice. The times are simulated.
512 devices in a mesh: field: 64 (over z, y), batch: 8 (over x, core).
Axes of the slice: x: 4, y: 8, z: 8, core: 2. Of those that a mesh axis runs over, the one named last changes fastest.
Arguments:
- pooled: bfloat16 [4096, 64, 1024], P('batch', 'field'), may hold values from -6 to 6
- counts: int32 [4096, 64], P('batch', 'field'), may hold values from 1 to 16
- w_pairs: bfloat16 [64, 504, 1024], P('field', None, 'batch'), may hold values from -0.03125 to 0.03125
- bias_terms: bfloat16 [1024], P('batch'), may hold values from -4 to 4
- grad_act: bfloat16 [4096, 1024], P('batch'), may hold values from -6 to 6
Outputs:
- entry_grad: bfloat16 [4096, 64, 1024], P('batch', 'field')
- weight_grad: float32 [64, 504, 1024], P('field', None, 'batch')
All inputs are finite; a program needn't handle non-finite values.
Results may differ from a plain program's by a relative error of at most 0.014.
Values may be sent and summed in bfloat16 or wider, within the bound.
No kernel may reach another device: no remote copies, remote signals or barrier semaphores. Data moves between devices by JAX's collectives and lax.ppermute only.
A program may use at most 64 MiB of HBM per device.

v0:
```python
import jax
import jax.numpy as jnp
from jax import lax
from jax.sharding import PartitionSpec as P


def body(pooled, counts, w_pairs, bias_terms, grad_act):
    sample_rows = pooled.shape[0]
    fields = lax.axis_size("field")
    shards = lax.axis_size("batch")
    depth = pooled.shape[2] // fields
    half_depth = depth // 2
    hidden_units = grad_act.shape[1]
    pair_count = w_pairs.shape[1]
    own_rows = sample_rows // fields
    my_field = lax.axis_index("field")
    f32, bf16 = (jnp.float32, jnp.bfloat16)
    embedded = pooled.reshape(sample_rows, fields, depth).transpose(1, 2, 0)
    partner = jnp.arange(fields, dtype=jnp.int32)[:, None, None]
    upper_half = partner < my_field
    mine = jnp.where(upper_half, embedded[:, half_depth:], embedded[:, :half_depth])
    outbound = jnp.where(upper_half, embedded[:, :half_depth], embedded[:, half_depth:])
    received = lax.all_to_all(outbound, "field", split_axis=0, concat_axis=0, tiled=True)
    bias_rows = jnp.pad(bias_terms[None, :], ((0, 0), (0, 0)))
    weight_bias = lax.all_gather(
        jnp.concatenate([w_pairs[0], bias_rows], 0), "batch", axis=1, tiled=True
    )
    weight_cols = weight_bias[:pair_count]
    bias_float = weight_bias[pair_count].astype(f32)
    received_wide = received.astype(f32)
    mine_wide = mine.astype(f32)
    product_all = (mine_wide * received_wide).astype(bf16)
    slot_index = jnp.arange(fields - 1, dtype=jnp.int32)[:, None, None]
    pair_rows = jnp.where(slot_index >= my_field, product_all[1:], product_all[:-1])
    pair_rows = pair_rows.reshape(pair_count, sample_rows)
    partial_hidden = lax.dot_general(
        pair_rows, weight_cols, (((0,), (0,)), ((), ())), preferred_element_type=f32
    )
    shares = lax.all_to_all(
        partial_hidden.astype(bf16).reshape(fields, own_rows, hidden_units),
        "field",
        split_axis=0,
        concat_axis=0,
        tiled=True,
    )
    preact = jnp.sum(shares.astype(f32), 0) + bias_float[None, :]
    gate_value = jax.nn.sigmoid(preact)
    own_grad = lax.dynamic_slice(grad_act, (my_field * own_rows, 0), (own_rows, hidden_units))
    own_slope = (own_grad.astype(f32) * gate_value * (1.0 + preact * (1.0 - gate_value))).astype(
        bf16
    )
    slope_act = lax.all_to_all(
        jnp.broadcast_to(own_slope[None], (fields, own_rows, hidden_units)),
        "field",
        split_axis=0,
        concat_axis=0,
        tiled=True,
    ).reshape(sample_rows, hidden_units)
    pair_grad = lax.dot_general(
        weight_cols, slope_act, (((1,), (1,)), ((), ())), preferred_element_type=f32
    ).reshape(fields - 1, half_depth, sample_rows)
    zero_slot = jnp.zeros((1, half_depth, sample_rows), f32)
    below_slots = jnp.concatenate([pair_grad, zero_slot], 0)
    above_slots = jnp.concatenate([zero_slot, pair_grad], 0)
    dense_grad = jnp.where(
        partner < my_field, below_slots, jnp.where(partner > my_field, above_slots, 0.0)
    )
    returned = lax.all_to_all(
        (dense_grad * mine_wide).astype(bf16), "field", split_axis=0, concat_axis=0, tiled=True
    ).astype(f32)
    weight_term = lax.dot_general(
        pair_rows, slope_act, (((1,), (0,)), ((), ())), preferred_element_type=f32
    ).astype(bf16)
    unit_cols = hidden_units // shards
    weight_shares = lax.all_to_all(
        weight_term.reshape(pair_count, shards, unit_cols).transpose(1, 0, 2),
        "batch",
        split_axis=0,
        concat_axis=0,
        tiled=True,
    )
    weight_grad = jnp.sum(weight_shares.astype(f32), 0)
    local_part = dense_grad * received_wide
    full_grad = jnp.concatenate(
        [jnp.where(upper_half, returned, local_part), jnp.where(upper_half, local_part, returned)],
        1,
    )
    full_grad = full_grad / jnp.sqrt(counts[:, 0].astype(f32))[None, None, :]
    entry_grad = full_grad.astype(bf16).reshape(fields * depth, sample_rows).T
    return (entry_grad[:, None, :], weight_grad[None])


def solution(mesh):
    in_specs = (
        P("batch", "field", None),
        P("batch", "field"),
        P("field", None, "batch"),
        P("batch"),
        P("batch", None),
    )
    out_specs = (P("batch", "field", None), P("field", None, "batch"))
    return jax.shard_map(body, mesh=mesh, in_specs=in_specs, out_specs=out_specs, check_vma=False)
```

profile of v0, /device:TPU:8, one launch (start us, length us, event | category | flops | bytes accessed | tf_op | source)
XLA Modules:
  0.0 168.9 jit_solution(5860360318695180854)
XLA Ops:
  0.7 1.5 copy.9
  2.2 0.9 broadcast_select_fusion
  3.2 16.6 %all-to-all-start = ((bf16[64,8,512]{2,1,0:T(8,128)(2,1)}), bf16[64,8,512]{2,1,0:T(8,128)(2,1)S(1)}, u32[]{:S(2)}, u32[]{:S(2)}) async-start(bf16[64,8,512]{2,1,0:T(8,128)(2,1)} %broadcast_select_fusion), calls=%async_computation | async-start | bytes 1048576 | tf_op jit(solution)/shard_map/all_to_all | solution.py:23
  19.8 14.6 %all_gather.3 = bf16[505,1024]{1,0:T(8,128)(2,1)S(1)} all-gather(bf16[505,128]{1,0:T(8,128)(2,1)S(1)} %pad_maximum_fusion.1), channel_id=1, replica_groups=mesh['field'=64,'batch'=8] {'batch'}, dimensions={1}, use_global_device_ids=true | all-gather | bytes 1163520 | tf_op jit(solution)/shard_map/all_gather | solution.py:25
  34.4 4.7 %all-to-all-done = bf16[64,8,512]{2,1,0:T(8,128)(2,1)S(1)} async-done(((bf16[64,8,512]{2,1,0:T(8,128)(2,1)}), bf16[64,8,512]{2,1,0:T(8,128)(2,1)S(1)}, u32[]{:S(2)}, u32[]{:S(2)}) %all-to-all-start) | async-done | bytes 524320 | tf_op jit(solution)/shard_map/all_to_all | solution.py:23
  39.1 0.3 fusion.3
  39.4 1.8 %fusion = bf16[64,8,1024]{2,1,0:T(8,128)(2,1)} fusion(bf16[505,1024]{1,0:T(8,128)(2,1)S(1)} %all_gather.3, bf16[64,8,512]{2,1,0:T(8,128)(2,1)S(1)} %fusion.3, pred[63]{0:T(512)(128)(4,1)S(1)} %iota_compare_fusion.1), kind=kOutput, calls=%fused_computation.6 | convolution fusion | flops 529264640 | bytes 3113472 | tf_op jit(solution)/shard_map/dot_general | solution.py:36
  41.2 8.0 %all-to-all-start.1 = ((bf16[64,8,1024]{2,1,0:T(8,128)(2,1)}), bf16[64,8,1024]{2,1,0:T(8,128)(2,1)S(1)}, u32[]{:S(2)}, u32[]{:S(2)}) async-start(bf16[64,8,1024]{2,1,0:T(8,128)(2,1)} %fusion), calls=%async_computation.1 | async-start | bytes 2097152 | tf_op jit(solution)/shard_map/all_to_all | solution.py:39
  49.2 0.7 slice_convert_fusion
  50.0 29.0 %all-to-all-done.1 = bf16[64,8,1024]{2,1,0:T(8,128)(2,1)S(1)} async-done(((bf16[64,8,1024]{2,1,0:T(8,128)(2,1)}), bf16[64,8,1024]{2,1,0:T(8,128)(2,1)S(1)}, u32[]{:S(2)}, u32[]{:S(2)}) %all-to-all-start.1) | async-done | bytes 1048608 | tf_op jit(solution)/shard_map/all_to_all | solution.py:39
  79.2 0.7 multiply_convert_fusion
  80.0 35.8 %all_to_all.25 = bf16[64,8,1024]{2,1,0:T(8,128)(2,1)S(1)} all-to-all(bf16[64,8,1024]{2,1,0:T(8,128)(2,1)S(1)} %broadcast_in_dim.66), channel_id=1, replica_groups=mesh['field'=64,'batch'=8] {'field'}, dimensions={0} | all-to-all | bytes 2097152 | tf_op jit(solution)/shard_map/all_to_all | solution.py:52
  115.9 0.7 fusion.1
  116.6 1.2 copy.14
  117.8 4.2 %all-to-all-start.4 = ((bf16[8,504,128]{2,1,0:T(8,128)(2,1)}), bf16[8,504,128]{2,1,0:T(8,128)(2,1)}, u32[]{:S(2)}, u32[]{:S(2)}) async-start(bf16[8,504,128]{2,1,0:T(8,128)(2,1)} %bitcast.36), calls=%async_computation.4 | async-start | bytes 2064384 | tf_op jit(solution)/shard_map/all_to_all | solution.py:75
  122.1 2.3 %fusion.4 = f32[63,8,512]{2,1,0:T(8,128)S(1)} fusion(bf16[64,8,1024]{2,1,0:T(8,128)(2,1)} %copy-done.1, bf16[505,1024]{1,0:T(8,128)(2,1)} %copy-done), kind=kOutput, calls=%fused_computation.15 | convolution fusion | flops 528482304 | bytes 3112960 | tf_op jit(solution)/shard_map/dot_general | solution.py:59
  124.4 1.1 fusion.2
  125.5 12.3 %all-to-all-done.4 = bf16[8,504,128]{2,1,0:T(8,128)(2,1)} async-done(((bf16[8,504,128]{2,1,0:T(8,128)(2,1)}), bf16[8,504,128]{2,1,0:T(8,128)(2,1)}, u32[]{:S(2)}, u32[]{:S(2)}) %all-to-all-start.4) | async-done | bytes 1032224 | tf_op jit(solution)/shard_map/all_to_all | solution.py:75
  137.8 6.7 %all-to-all-start.3 = ((bf16[64,8,512]{2,1,0:T(8,128)(2,1)}), bf16[64,8,512]{2,1,0:T(8,128)(2,1)S(1)}, u32[]{:S(2)}, u32[]{:S(2)}) async-start(bf16[64,8,512]{2,1,0:T(8,128)(2,1)} %fusion.2), calls=%async_computation.3 | async-start | bytes 1048576 | tf_op jit(solution)/shard_map/all_to_all | solution.py:68
  144.5 2.1 %convert_reduce_fusion.1 = f32[504,128]{1,0:T(8,128)} fusion(bf16[8,504,128]{2,1,0:T(8,128)(2,1)} %all-to-all-done.4), kind=kLoop, calls=%fused_computation.3 | loop fusion | flops 967680 | bytes 1290240 | tf_op jit(solution)/shard_map/reduce_sum | solution.py:82
  146.6 17.0 %all-to-all-done.3 = bf16[64,8,512]{2,1,0:T(8,128)(2,1)S(1)} async-done(((bf16[64,8,512]{2,1,0:T(8,128)(2,1)}), bf16[64,8,512]{2,1,0:T(8,128)(2,1)S(1)}, u32[]{:S(2)}, u32[]{:S(2)}) %all-to-all-start.3) | async-done | bytes 524320 | tf_op jit(solution)/shard_map/all_to_all | solution.py:68
  163.6 0.4 convert_select_fusion.1
  164.2 1.9 %copy.10 = f32[1024,512]{0,1:T(8,128)} copy(f32[1024,512]{1,0:T(8,128)S(1)} %bitcast.40) | data formatting | bytes 4194304 | tf_op jit(solution)/shard_map/concatenate | solution.py:84
  166.0 2.8 %fusion.7 = bf16[512,1,1024]{2,0,1:T(8,128)(2,1)} fusion(f32[1024,512]{0,1:T(8,128)} %copy.10, f32[512]{0:T(512)S(1)} %bitcast.44), kind=kLoop, calls=%fused_computation.19 | loop fusion | flops 1048576 | bytes 3147776 | tf_op jit(solution)/shard_map/broadcast_in_dim | solution.py:90
  (18 shorter events, 0.6 us)
Async XLA Ops:
  0.6 19.1 %copy-start.2 = (bf16[1,504,128]{2,1,0:T(8,128)(2,1)S(1)}, bf16[1,504,128]{2,1,0:T(8,128)(2,1)}, u32[]{:S(2)}) copy-start(bf16[1,504,128]{2,1,0:T(8,128)(2,1)} %param.7) | copy-start | bytes 387076
  0.7 19.1 %copy-start.4 = (bf16[128]{0:T(256)(128)(2,1)S(1)}, bf16[128]{0:T(256)(128)(2,1)}, u32[]{:S(2)}) copy-start(bf16[128]{0:T(256)(128)(2,1)} %param.8) | copy-start | bytes 772
  3.2 36.0 %all-to-all-start = ((bf16[64,8,512]{2,1,0:T(8,128)(2,1)}), bf16[64,8,512]{2,1,0:T(8,128)(2,1)S(1)}, u32[]{:S(2)}, u32[]{:S(2)}) async-start(bf16[64,8,512]{2,1,0:T(8,128)(2,1)} %broadcast_select_fusion), calls=%async_computation | async-start | bytes 1048576 | tf_op jit(solution)/shard_map/all_to_all | solution.py:23
  34.4 6.8 %copy-start = (bf16[505,1024]{1,0:T(8,128)(2,1)}, bf16[505,1024]{1,0:T(8,128)(2,1)S(1)}, u32[]{:S(2)}) copy-start(bf16[505,1024]{1,0:T(8,128)(2,1)S(1)} %all_gather.3) | copy-start | bytes 3102724
  41.2 37.8 %all-to-all-start.1 = ((bf16[64,8,1024]{2,1,0:T(8,128)(2,1)}), bf16[64,8,1024]{2,1,0:T(8,128)(2,1)S(1)}, u32[]{:S(2)}, u32[]{:S(2)}) async-start(bf16[64,8,1024]{2,1,0:T(8,128)(2,1)} %fusion), calls=%async_computation.1 | async-start | bytes 2097152 | tf_op jit(solution)/shard_map/all_to_all | solution.py:39
  115.9 1.9 %copy-start.1 = (bf16[64,8,1024]{2,1,0:T(8,128)(2,1)}, bf16[64,8,1024]{2,1,0:T(8,128)(2,1)S(1)}, u32[]{:S(2)}) copy-start(bf16[64,8,1024]{2,1,0:T(8,128)(2,1)S(1)} %all_to_all.25) | copy-start | bytes 3145732
  117.8 20.0 %all-to-all-start.4 = ((bf16[8,504,128]{2,1,0:T(8,128)(2,1)}), bf16[8,504,128]{2,1,0:T(8,128)(2,1)}, u32[]{:S(2)}, u32[]{:S(2)}) async-start(bf16[8,504,128]{2,1,0:T(8,128)(2,1)} %bitcast.36), calls=%async_computation.4 | async-start | bytes 2064384 | tf_op jit(solution)/shard_map/all_to_all | solution.py:75
  124.3 20.1 %copy-start.3 = (s32[512,1]{0,1:T(1,128)S(1)}, s32[512,1]{0,1:T(1,128)}, u32[]{:S(2)}) copy-start(s32[512,1]{0,1:T(1,128)} %param.6) | copy-start | bytes 6148
  137.8 25.8 %all-to-all-start.3 = ((bf16[64,8,512]{2,1,0:T(8,128)(2,1)}), bf16[64,8,512]{2,1,0:T(8,128)(2,1)S(1)}, u32[]{:S(2)}, u32[]{:S(2)}) async-start(bf16[64,8,512]{2,1,0:T(8,128)(2,1)} %fusion.2), calls=%async_computation.3 | async-start | bytes 1048576 | tf_op jit(solution)/shard_map/all_to_all | solution.py:68
where the time goes:
time: 170 us; the launch traced here: 169 us
  waiting for transfers between devices  63 us (37%)
  blocking collectives  50.5 us (30%)
  starting transfers between devices  35.5 us (21%)
  other arithmetic  9.48 us (6%)
  matrix products  4.84 us (3%)
  local copies, waits for them, and re-layouts  4.73 us (3%)
    all_to_all x1, blocking collectives, body(): lax.all_to_all(jnp.broadcast_to(own_slope[None], (fields, own_rows, hidde...  35.8 us
    all_to_all x1, waiting for transfers between devices, body(): lax.all_to_all(partial_hidden.astype(bf16).reshape(fields, own_rows, hidd...  29 us
    all_to_all x1, waiting for transfers between devices, body(): lax.all_to_all((dense_grad * mine_wide).astype(bf16), 'field', split_axis...  17 us
    all_to_all x1, starting transfers between devices, body(): lax.all_to_all(outbound, 'field', split_axis=0, concat_axis=0, tiled=True)  16.6 us
    all_gather x1, blocking collectives, body(): lax.all_gather(jnp.concatenate([w_pairs[0], bias_rows], 0), 'batch', axis...  14.6 us
    all_to_all x1, waiting for transfers between devices, body(): lax.all_to_all(weight_term.reshape(pair_count, shards, unit_cols).transpo...  12.3 us
    all_to_all x1, starting transfers between devices, body(): lax.all_to_all(partial_hidden.astype(bf16).reshape(fields, own_rows, hidd...  8.01 us
    all_to_all x1, starting transfers between devices, body(): lax.all_to_all((dense_grad * mine_wide).astype(bf16), 'field', split_axis...  6.67 us
  transfers between devices with their start and end apart: 4, of which 4 were waited for; matrix products, arithmetic and copies ran while one was open for 4% of the time, Pallas kernels for 0%

commit v1 on v0

--- a/solution.py
+++ b/solution.py
@@ -22,9 +22,9 @@
     outbound = jnp.where(upper_half, embedded[:, :half_depth], embedded[:, half_depth:])
     received = lax.all_to_all(outbound, "field", split_axis=0, concat_axis=0, tiled=True)
     bias_rows = jnp.pad(bias_terms[None, :], ((0, 0), (0, 0)))
-    weight_bias = lax.all_gather(
-        jnp.concatenate([w_pairs[0], bias_rows], 0), "batch", axis=1, tiled=True
-    )
+    block = jnp.concatenate([w_pairs[0], bias_rows], 0)
+    sent = jnp.stack([block] * lax.axis_size("batch"))
+    weight_bias = jnp.concatenate(lax.all_to_all(sent, "batch", 0, 0), axis=1)
     weight_cols = weight_bias[:pair_count]
     bias_float = weight_bias[pair_count].astype(f32)
     received_wide = received.astype(f32)

time: 170 us -> 187 us (1.10)
  waiting for transfers between devices: 63 us -> 84.6 us
  blocking collectives: 50.5 us -> 34.6 us
  local copies, waits for them, and re-layouts: 4.73 us -> 11.8 us
  other arithmetic: 9.48 us -> 11.7 us
    all_gather x1 -> x0, blocking collectives: 14.6 us -> none  [body(): lax.all_gather(jnp.concatenate([w_pairs[0], bias_rows], 0), 'batch', axis...]
    all_to_all x0 -> x1, waiting for transfers between devices: none -> 14.5 us  [body(): weight_bias = jnp.concatenate(lax.all_to_all(sent, 'batch', 0, 0), axis=1)]
    all_to_all x1, waiting for transfers between devices: 4.7 us -> 16.5 us  [body(): lax.all_to_all(outbound, 'field', split_axis=0, concat_axis=0, tiled=True)]
    all_to_all x0 -> x1, starting transfers between devices: none -> 4.3 us  [body(): weight_bias = jnp.concatenate(lax.all_to_all(sent, 'batch', 0, 0), axis=1)]
    slice x0 -> x3, local copies, waits for them, and re-layouts: none -> 3.73 us  [body(): weight_cols = weight_bias[:pair_count]]
    all_to_all x1, waiting for transfers between devices: 12.3 us -> 8.9 us  [body(): lax.all_to_all(weight_term.reshape(pair_count, shards, unit_cols).transpo...]
    all_to_all x1, starting transfers between devices: 8.01 us -> 5.62 us  [body(): lax.all_to_all(partial_hidden.astype(bf16).reshape(fields, own_rows, hidd...]
    dot_general x0 -> x1, local copies, waits for them, and re-layouts: none -> 2.31 us  [body(): lax.dot_general(weight_cols, slope_act, (((1,), (1,)), ((), ())), preferr...]
  transfers between devices with their start and end apart: 4 -> 5, of which waited for: 4 -> 5; matrix products, arithmetic and copies ran while one was open for 4% -> 7% of each run, Pallas kernels for 0% -> 0%
where the time goes in v1:
time: 187 us; the launch traced here: 186 us
  waiting for transfers between devices  84.6 us (45%)
  starting transfers between devices  37.3 us (20%)
  blocking collectives  34.6 us (19%)
  local copies, waits for them, and re-layouts  11.8 us (6%)
  other arithmetic  11.7 us (6%)
  matrix products  4.92 us (3%)
    all_to_all x1, blocking collectives, body(): lax.all_to_all(jnp.broadcast_to(own_slope[None], (fields, own_rows, hidde...  34.6 us
    all_to_all x1, waiting for transfers between devices, body(): lax.all_to_all(partial_hidden.astype(bf16).reshape(fields, own_rows, hidd...  27.7 us
    all_to_all x1, waiting for transfers between devices, body(): lax.all_to_all((dense_grad * mine_wide).astype(bf16), 'field', split_axis...  17 us
    all_to_all x1, starting transfers between devices, body(): lax.all_to_all(outbound, 'field', split_axis=0, concat_axis=0, tiled=True)  16.6 us
    all_to_all x1, waiting for transfers between devices, body(): lax.all_to_all(outbound, 'field', split_axis=0, concat_axis=0, tiled=True)  16.5 us
    all_to_all x1, waiting for transfers between devices, body(): weight_bias = jnp.concatenate(lax.all_to_all(sent, 'batch', 0, 0), axis=1)  14.5 us
    all_to_all x1, waiting for transfers between devices, body(): lax.all_to_all(weight_term.reshape(pair_count, shards, unit_cols).transpo...  8.9 us
    all_to_all x1, starting transfers between devices, body(): lax.all_to_all((dense_grad * mine_wide).astype(bf16), 'field', split_axis...  6.55 us
  transfers between devices with their start and end apart: 5, of which 5 were waited for; matrix products, arithmetic and copies ran while one was open for 7% of the time, Pallas kernels for 0%

profile of v1, /device:TPU:8, one launch (start us, length us, event | category | flops | bytes accessed | tf_op | source)
XLA Modules:
  0.0 185.8 jit_solution(172808702459877028)
XLA Ops:
  1.7 1.1 stack.2
  2.8 4.3 %all-to-all-start = ((bf16[8,505,128]{2,1,0:T(8,128)(2,1)}), bf16[8,505,128]{2,1,0:T(8,128)(2,1)}, u32[]{:S(2)}, u32[]{:S(2)}) async-start(bf16[8,505,128]{2,1,0:T(8,128)(2,1)} %stack.2), calls=%async_computation | async-start | bytes 2097152 | tf_op jit(solution)/shard_map/all_to_all | solution.py:27
  8.6 14.5 %all-to-all-done = bf16[8,505,128]{2,1,0:T(8,128)(2,1)} async-done(((bf16[8,505,128]{2,1,0:T(8,128)(2,1)}), bf16[8,505,128]{2,1,0:T(8,128)(2,1)}, u32[]{:S(2)}, u32[]{:S(2)}) %all-to-all-start) | async-done | bytes 1034272 | tf_op jit(solution)/shard_map/all_to_all | solution.py:27
  23.1 16.6 %all-to-all-start.1 = ((bf16[64,8,512]{2,1,0:T(8,128)(2,1)}), bf16[64,8,512]{2,1,0:T(8,128)(2,1)S(1)}, u32[]{:S(2)}, u32[]{:S(2)}) async-start(bf16[64,8,512]{2,1,0:T(8,128)(2,1)} %broadcast_select_fusion), calls=%async_computation.1 | async-start | bytes 1048576 | tf_op jit(solution)/shard_map/all_to_all | solution.py:23
  39.7 1.3 slice.31
  41.0 1.3 copy.15
  42.3 16.5 %all-to-all-done.1 = bf16[64,8,512]{2,1,0:T(8,128)(2,1)S(1)} async-done(((bf16[64,8,512]{2,1,0:T(8,128)(2,1)}), bf16[64,8,512]{2,1,0:T(8,128)(2,1)S(1)}, u32[]{:S(2)}, u32[]{:S(2)}) %all-to-all-start.1) | async-done | bytes 524320 | tf_op jit(solution)/shard_map/all_to_all | solution.py:23
  60.0 1.9 %fusion = bf16[64,8,1024]{2,1,0:T(8,128)(2,1)} fusion(bf16[504,1024]{0,1:T(8,128)(2,1)S(1)} %bitcast.43, bf16[64,8,512]{2,1,0:T(8,128)(2,1)S(1)} %fusion.3, pred[63]{0:T(512)(128)(4,1)S(1)} %iota_compare_fusion.1), kind=kOutput, calls=%fused_computation.6 | convolution fusion | flops 529264640 | bytes 3129856 | tf_op jit(solution)/shard_map/dot_general | solution.py:36
  61.9 5.6 %all-to-all-start.2 = ((bf16[64,8,1024]{2,1,0:T(8,128)(2,1)}), bf16[64,8,1024]{2,1,0:T(8,128)(2,1)}, u32[]{:S(2)}, u32[]{:S(2)}) async-start(bf16[64,8,1024]{2,1,0:T(8,128)(2,1)} %fusion), calls=%async_computation.2 | async-start | bytes 2097152 | tf_op jit(solution)/shard_map/all_to_all | solution.py:39
  68.3 27.7 %all-to-all-done.2 = bf16[64,8,1024]{2,1,0:T(8,128)(2,1)} async-done(((bf16[64,8,1024]{2,1,0:T(8,128)(2,1)}), bf16[64,8,1024]{2,1,0:T(8,128)(2,1)}, u32[]{:S(2)}, u32[]{:S(2)}) %all-to-all-start.2) | async-done | bytes 1048608 | tf_op jit(solution)/shard_map/all_to_all | solution.py:39
  96.0 1.4 convert_reduce_fusion
  98.3 34.6 %all_to_all.30 = bf16[64,8,1024]{2,1,0:T(8,128)(2,1)S(1)} all-to-all(bf16[64,8,1024]{2,1,0:T(8,128)(2,1)S(1)} %broadcast_in_dim.66), channel_id=1, replica_groups=mesh['field'=64,'batch'=8] {'field'}, dimensions={0} | all-to-all | bytes 2097152 | tf_op jit(solution)/shard_map/all_to_all | solution.py:52
  133.7 1.2 copy.20
  134.9 4.2 %all-to-all-start.5 = ((bf16[8,504,128]{2,1,0:T(8,128)(2,1)}), bf16[8,504,128]{2,1,0:T(8,128)(2,1)}, u32[]{:S(2)}, u32[]{:S(2)}) async-start(bf16[8,504,128]{2,1,0:T(8,128)(2,1)} %bitcast.42), calls=%async_computation.5 | async-start | bytes 2064384 | tf_op jit(solution)/shard_map/all_to_all | solution.py:75
  139.1 1.1 copy.13
  140.3 2.3 %dot_general.11 = bf16[63,8,1024]{2,1,0:T(8,128)(2,1)} reshape(bf16[504,8,128]{2,1,0:T(8,128)(2,1)} %copy.13) | data formatting | bytes 2064384 | tf_op jit(solution)/shard_map/dot_general | solution.py:59
  142.6 2.3 %fusion.4 = f32[63,8,512]{2,1,0:T(8,128)S(1)} fusion(bf16[63,8,1024]{2,1,0:T(8,128)(2,1)} %dot_general.11, bf16[64,8,1024]{2,1,0:T(8,128)(2,1)} %copy-done.1), kind=kOutput, calls=%fused_computation.15 | convolution fusion | flops 528482304 | bytes 3112960 | tf_op jit(solution)/shard_map/dot_general | solution.py:59
  144.9 1.1 fusion.2
  146.0 8.9 %all-to-all-done.5 = bf16[8,504,128]{2,1,0:T(8,128)(2,1)} async-done(((bf16[8,504,128]{2,1,0:T(8,128)(2,1)}), bf16[8,504,128]{2,1,0:T(8,128)(2,1)}, u32[]{:S(2)}, u32[]{:S(2)}) %all-to-all-start.5) | async-done | bytes 1032224 | tf_op jit(solution)/shard_map/all_to_all | solution.py:75
  154.9 6.5 %all-to-all-start.4 = ((bf16[64,8,512]{2,1,0:T(8,128)(2,1)}), bf16[64,8,512]{2,1,0:T(8,128)(2,1)S(1)}, u32[]{:S(2)}, u32[]{:S(2)}) async-start(bf16[64,8,512]{2,1,0:T(8,128)(2,1)} %fusion.2), calls=%async_computation.4 | async-start | bytes 1048576 | tf_op jit(solution)/shard_map/all_to_all | solution.py:68
  161.5 2.1 %convert_reduce_fusion.1 = f32[504,128]{1,0:T(8,128)} fusion(bf16[8,504,128]{2,1,0:T(8,128)(2,1)} %all-to-all-done.5), kind=kLoop, calls=%fused_computation.3 | loop fusion | flops 967680 | bytes 1290240 | tf_op jit(solution)/shard_map/reduce_sum | solution.py:82
  163.5 17.0 %all-to-all-done.4 = bf16[64,8,512]{2,1,0:T(8,128)(2,1)S(1)} async-done(((bf16[64,8,512]{2,1,0:T(8,128)(2,1)}), bf16[64,8,512]{2,1,0:T(8,128)(2,1)S(1)}, u32[]{:S(2)}, u32[]{:S(2)}) %all-to-all-start.4) | async-done | bytes 524320 | tf_op jit(solution)/shard_map/all_to_all | solution.py:68
  181.1 1.9 %copy.16 = f32[1024,512]{0,1:T(8,128)} copy(f32[1024,512]{1,0:T(8,128)S(1)} %bitcast.41) | data formatting | bytes 4194304 | tf_op jit(solution)/shard_map/concatenate | solution.py:84
  183.0 2.8 %fusion.7 = bf16[512,1,1024]{2,0,1:T(8,128)(2,1)} fusion(f32[1024,512]{0,1:T(8,128)} %copy.16, f32[512]{0:T(512)S(1)} %bitcast.47), kind=kLoop, calls=%fused_computation.19 | loop fusion | flops 1048576 | bytes 3147776 | tf_op jit(solution)/shard_map/broadcast_in_dim | solution.py:90
  (22 shorter events, 6.7 us)
Async XLA Ops:
  0.6 6.4 %copy-start = (bf16[512,1,1024]{2,0,1:T(8,128)(2,1)S(1)}, bf16[512,1,1024]{2,0,1:T(8,128)(2,1)}, u32[]{:S(2)}) copy-start(bf16[512,1,1024]{2,0,1:T(8,128)(2,1)} %param.5) | copy-start | bytes 3145732
  2.8 20.3 %all-to-all-start = ((bf16[8,505,128]{2,1,0:T(8,128)(2,1)}), bf16[8,505,128]{2,1,0:T(8,128)(2,1)}, u32[]{:S(2)}, u32[]{:S(2)}) async-start(bf16[8,505,128]{2,1,0:T(8,128)(2,1)} %stack.2), calls=%async_computation | async-start | bytes 2097152 | tf_op jit(solution)/shard_map/all_to_all | solution.py:27
  23.1 35.7 %all-to-all-start.1 = ((bf16[64,8,512]{2,1,0:T(8,128)(2,1)}), bf16[64,8,512]{2,1,0:T(8,128)(2,1)S(1)}, u32[]{:S(2)}, u32[]{:S(2)}) async-start(bf16[64,8,512]{2,1,0:T(8,128)(2,1)} %broadcast_select_fusion), calls=%async_computation.1 | async-start | bytes 1048576 | tf_op jit(solution)/shard_map/all_to_all | solution.py:23
  58.8 1.2 copy-start.2
  61.9 34.1 %all-to-all-start.2 = ((bf16[64,8,1024]{2,1,0:T(8,128)(2,1)}), bf16[64,8,1024]{2,1,0:T(8,128)(2,1)}, u32[]{:S(2)}, u32[]{:S(2)}) async-start(bf16[64,8,1024]{2,1,0:T(8,128)(2,1)} %fusion), calls=%async_computation.2 | async-start | bytes 2097152 | tf_op jit(solution)/shard_map/all_to_all | solution.py:39
  132.9 2.0 %copy-start.1 = (bf16[64,8,1024]{2,1,0:T(8,128)(2,1)}, bf16[64,8,1024]{2,1,0:T(8,128)(2,1)S(1)}, u32[]{:S(2)}) copy-start(bf16[64,8,1024]{2,1,0:T(8,128)(2,1)S(1)} %all_to_all.30) | copy-start | bytes 3145732
  134.9 20.0 %all-to-all-start.5 = ((bf16[8,504,128]{2,1,0:T(8,128)(2,1)}), bf16[8,504,128]{2,1,0:T(8,128)(2,1)}, u32[]{:S(2)}, u32[]{:S(2)}) async-start(bf16[8,504,128]{2,1,0:T(8,128)(2,1)} %bitcast.42), calls=%async_computation.5 | async-start | bytes 2064384 | tf_op jit(solution)/shard_map/all_to_all | solution.py:75
  144.8 16.6 %copy-start.3 = (s32[512,1]{0,1:T(1,128)S(1)}, s32[512,1]{0,1:T(1,128)}, u32[]{:S(2)}) copy-start(s32[512,1]{0,1:T(1,128)} %param.6) | copy-start | bytes 6148
  154.9 25.6 %all-to-all-start.4 = ((bf16[64,8,512]{2,1,0:T(8,128)(2,1)}), bf16[64,8,512]{2,1,0:T(8,128)(2,1)S(1)}, u32[]{:S(2)}, u32[]{:S(2)}) async-start(bf16[64,8,512]{2,1,0:T(8,128)(2,1)} %fusion.2), calls=%async_computation.4 | async-start | bytes 1048576 | tf_op jit(solution)/shard_map/all_to_all | solution.py:68
